TPU v7x, 32 devices: a whole 2x2x4 slice. The times are simulated.
32 devices in a mesh: groups: 2 (over x), span: 8 (over z, y), head: 2 (over core).
Axes of the slice: x: 2, y: 2, z: 4, core: 2. Of those that a mesh axis runs over, the one named last changes fastest.
Arguments:
- span_states: bfloat16 [2048, 4096], P(('groups', 'span'), 'head'), parts along dimension 0, may hold values from -1.5 to 1.5
- span_queries: bfloat16 [2048, 2048], P(('groups', 'span'), 'head'), parts along dimension 0, may hold values from -1000 to 1000
- span_memory: bfloat16 [2048, 2, 896], P(('groups', 'span'), None, 'head'), parts along dimension 0, may hold values from -1000 to 1000
- passages: bfloat16 [16384, 896], P(('groups', 'span')), parts along dimension 0, may hold values from -1.5 to 1.5
- neighbours: int32 [32, 2], P(('groups', 'span')), parts along dimension 0, may hold values from 0 to 63, as said below
- enc_query_w: bfloat16 [896, 896], P(None, 'head'), may hold values from -0.1875 to 0.1875
- enc_out_w: bfloat16 [896, 896], P(None, 'head'), may hold values from -0.1875 to 0.1875
- kv_weight: bfloat16 [896, 2, 2048], P(None, None, ('head', 'span')), may hold values from -0.1875 to 0.1875
- out_weight: bfloat16 [2048, 4096], P('head', 'span'), may hold values from -0.125 to 0.125
Outputs:
- mixed_states: bfloat16 [2048, 4096], P(('groups', 'span'), 'head'), parts along dimension 0
There are 2 independent parts, one for each index of `groups`. A program takes and returns all parts, laid end to end along the dimension named above; an argument that names none is the same for every part. Nothing has to cross between parts.
Inputs may be any that keep to these rules, and one draw needn't show every extreme that they name: `neighbours`: passage p belongs to index p // 8 of the span axis. Among the spans of one index of the span axis, all 4 passages listed belong to distinct indices.
All inputs are finite; a program needn't handle non-finite values.
Results may differ from a plain program's by a relative error of at most 0.025.
Values may be sent and summed in bfloat16 or wider, within the bound.
A program may use at most 64 MiB of HBM per device.

v0:
```python
import math
import jax
import jax.numpy as jnp
from jax import lax
from jax.sharding import PartitionSpec as P

HD = 128
E = 896
EHD = 64
CT = 64
PT = 128
NB = 2
PS_DEV = 8
epsilon = 1e-06


def rms_rows(values):
    return values * lax.rsqrt(jnp.mean(values * values, axis=-1, keepdims=True) + epsilon)


def softmax_rows(scores):
    top_score = jnp.max(scores, axis=-1, keepdims=True)
    raised = jnp.exp(scores - top_score)
    return raised / jnp.sum(raised, axis=-1, keepdims=True)


def wanted_slots(owner_flat, local_flat, device_count):
    matched = owner_flat[:, None] == jnp.arange(device_count, dtype=jnp.int32)[None, :]
    return jnp.sum(jnp.where(matched, local_flat[:, None], 0), axis=0)


def fetch_passages(wanted, passages):
    blocks = passages.reshape(-1, PT, E)
    picked = blocks[lax.all_to_all(wanted, "span", split_axis=0, concat_axis=0, tiled=True)]
    return lax.all_to_all(picked, "span", split_axis=0, concat_axis=0, tiled=True)


def encode_branch(copies, memory, query_w, out_w):
    groups = copies.shape[0]
    span_count = copies.shape[1]
    head_count = memory.shape[3]
    flat_rows = copies.reshape(-1, E).astype(jnp.float32)
    normed = rms_rows(flat_rows).astype(jnp.bfloat16)
    enc_query = jnp.dot(normed, query_w, preferred_element_type=jnp.float32).astype(jnp.bfloat16)
    enc_query = enc_query.reshape(groups, span_count, PT, head_count, EHD)
    scores = jnp.einsum(
        "gcqhd,ckhd->gchqk", enc_query, memory[:, :, 0], preferred_element_type=jnp.float32
    ) / math.sqrt(EHD)
    weights = softmax_rows(scores).astype(jnp.bfloat16)
    mixed_heads = jnp.einsum(
        "gchqk,ckhd->gcqhd", weights, memory[:, :, 1], preferred_element_type=jnp.float32
    )
    mixed_heads = mixed_heads.astype(jnp.bfloat16).reshape(-1, head_count * EHD)
    branch = lax.dot_general(
        mixed_heads, out_w, (((1,), (1,)), ((), ())), preferred_element_type=jnp.float32
    )
    return (flat_rows, branch)


def body(
    span_states,
    span_queries,
    span_memory,
    passages,
    neighbours,
    enc_query_w,
    enc_out_w,
    kv_weight,
    out_weight,
):
    device_count = lax.axis_size("span")
    head_index = lax.axis_index("head")
    span_count = neighbours.shape[0]
    owners = neighbours // PS_DEV
    local_ids = neighbours % PS_DEV
    wanted = wanted_slots(owners.reshape(-1), local_ids.reshape(-1), device_count)[:, None]
    fetched = fetch_passages(wanted, passages)
    own_owner = lax.dynamic_index_in_dim(owners, head_index, 1, keepdims=False)
    copies = fetched[own_owner, 0][None]
    query_full, out_full = (
        lax.all_gather(enc_query_w, "head", axis=1, tiled=True),
        lax.all_gather(enc_out_w, "head", axis=1, tiled=True),
    )
    memory_full = lax.all_gather(span_memory, "head", axis=2, tiled=True)
    memory = memory_full.reshape(span_count, CT, 2, -1, EHD)
    own_rows, own_branch = encode_branch(copies, memory, query_full, out_full)
    encoded = rms_rows(own_rows + own_branch).astype(jnp.bfloat16)
    all_encoded = lax.all_gather(encoded[None], "head", axis=0, tiled=True)
    flat_encoded = all_encoded.reshape(-1, E)
    dec_kv = jnp.einsum(
        "re,esc->rsc",
        flat_encoded,
        lax.all_gather(kv_weight, "span", axis=2, tiled=True),
        preferred_element_type=jnp.float32,
    ).astype(jnp.bfloat16)
    head_count = span_queries.shape[1] // HD
    dec_kv = dec_kv.reshape(NB, span_count, PT, 2, head_count, HD)
    dec_query = span_queries.reshape(span_count, CT, head_count, HD)
    scores = jnp.einsum(
        "cqhd,ncphd->chqnp", dec_query, dec_kv[:, :, :, 0], preferred_element_type=jnp.float32
    ) / math.sqrt(HD)
    scores = scores.reshape(span_count, head_count, CT, NB * PT)
    weights = softmax_rows(scores).astype(jnp.bfloat16).reshape(span_count, head_count, CT, NB, PT)
    attended = jnp.einsum(
        "chqnp,ncphd->cqhd", weights, dec_kv[:, :, :, 1], preferred_element_type=jnp.float32
    )
    attended = attended.astype(jnp.bfloat16).reshape(span_count * CT, head_count * HD)
    partial_value = jnp.dot(
        attended,
        lax.all_gather(out_weight, "span", axis=1, tiled=True),
        preferred_element_type=jnp.float32,
    )
    summed = lax.psum_scatter(
        partial_value.astype(jnp.bfloat16), "head", scatter_dimension=1, tiled=True
    ).astype(jnp.float32)
    return (span_states.astype(jnp.float32) + summed).astype(jnp.bfloat16)


def solution(mesh):
    placed = (
        P(("groups", "span"), "head"),
        P(("groups", "span"), "head"),
        P(("groups", "span"), None, "head"),
        P(("groups", "span"), None),
        P(("groups", "span"), None),
        P(None, "head"),
        P(None, "head"),
        P(None, None, ("head", "span")),
        P("head", "span"),
    )
    return jax.shard_map(
        body, mesh=mesh, in_specs=placed, out_specs=P(("groups", "span"), "head"), check_vma=False
    )
```

profile of v0, /device:TPU:0, one launch (start us, length us, event | category | flops | bytes accessed | tf_op | source)
XLA Modules:
  0.0 270.7 jit_solution(14112811568693671814)
XLA Ops:
  6.5 0.7 all-gather.6.cloned.1.call-update
  7.3 0.0 all-gather.8.cloned.1.call-start
  7.3 0.7 all-gather.8.cloned.1.call-update
  8.0 0.0 all-gather.10.cloned.1.call-start
  8.1 0.8 copy.54
  8.9 0.0 all-gather.12.cloned.1.call-start
  9.0 0.5 all-gather.12.cloned.1.call-update
  9.5 0.1 eq.17
  9.6 0.1 broadcast_in_dim.16
  9.7 0.1 select_reduce_fusion
  9.8 0.1 copy.48
  9.9 13.6 %all_to_all.14 = s32[8,1,1]{2,1,0:T(1,128)S(1)} all-to-all(s32[8,1,1]{2,1,0:T(1,128)S(1)} %copy.48), channel_id=1, replica_groups=mesh['groups'=2,'span'=8,'head'=2] {'span'}, dimensions={0} | all-to-all | bytes 64 | tf_op jit(solution)/shard_map/all_to_all | solution.py:34
  23.5 0.2 fusion.20
  23.7 2.0 gather_fusion
  25.7 4.4 %all-to-all-start.1 = ((bf16[8,1,128,896]{3,2,1,0:T(8,128)(2,1)}), bf16[8,1,128,896]{3,2,1,0:T(8,128)(2,1)}, u32[]{:S(2)}, u32[]{:S(2)}) async-start(bf16[8,1,128,896]{3,2,1,0:T(8,128)(2,1)} %bitcast.92), calls=%async_computation.1 | async-start | bytes 3670016 | tf_op jit(solution)/shard_map/all_to_all | solution.py:35
  30.2 0.0 reduce-scatter.2.cloned.1.call-start
  30.2 2.1 all_gather.19
  32.4 0.4 reshape.91
  32.8 1.7 fusion.25
  34.4 1.1 copy.66
  35.6 0.2 fusion.23
  35.8 0.7 bitcast_bitcast_fusion
  36.5 49.9 %all-to-all-done.1 = bf16[8,1,128,896]{3,2,1,0:T(8,128)(2,1)} async-done(((bf16[8,1,128,896]{3,2,1,0:T(8,128)(2,1)}), bf16[8,1,128,896]{3,2,1,0:T(8,128)(2,1)}, u32[]{:S(2)}, u32[]{:S(2)}) %all-to-all-start.1) | async-done | bytes 1835040 | tf_op jit(solution)/shard_map/all_to_all | solution.py:35
  86.4 2.1 gather_fusion.1
  88.5 0.2 multiply_reduce_fusion.1
  88.7 0.1 fusion.8
  88.9 3.0 %convolution_convert_fusion.3 = bf16[256,896]{1,0:T(8,128)(2,1)} fusion(bf16[256,896]{1,0:T(8,128)(2,1)S(1)} %fusion.8, bf16[896,896]{0,1:T(8,128)(2,1)} %all-gather.6.cloned.1.call-done), kind=kOutput, calls=%fused_computation.10 | convolution fusion | flops 411271168 | bytes 2523136 | tf_op jit(solution)/shard_map/dot_general | solution.py:44
  91.9 1.8 reshape.118
  93.7 1.8 fusion.26
  95.5 0.2 fusion.9
  95.7 0.3 fusion.2
  96.0 0.5 copy.53
  96.5 2.2 multiply_reduce_fusion
  98.8 0.1 multiply_convert_fusion
  98.9 2.5 all-gather
  101.4 23.2 %all-gather.10.cloned.1.call-done = bf16[896,2,1024]{2,0,1:T(8,128)(2,1)} async-done(((bf16[896,2,128]{2,0,1:T(8,128)(2,1)}), bf16[896,2,1024]{2,0,1:T(8,128)(2,1)}) %all-gather.10.cloned.1.call-update) | async-done | bytes 3670032 | tf_op jit(solution)/shard_map/all_gather | solution.py:93
  124.5 4.4 %convolution_convert_fusion.1 = bf16[512,2,1024]{2,0,1:T(8,128)(2,1)S(1)} fusion(bf16[896,2,1024]{2,0,1:T(8,128)(2,1)} %all-gather.10.cloned.1.call-done, bf16[512,896]{1,0:T(8,128)(2,1)S(1)} %all-gather), kind=kOutput, calls=%fused_computation.3 | convolution fusion | flops 1880096768 | bytes 6684672 | tf_op jit(solution)/shard_map/re,esc->rsc/dot_general | solution.py:90
  128.9 0.6 copy.70
  129.5 0.1 fusion.24
  129.7 0.8 copy-done.1
  130.5 0.6 fusion.27
  131.1 0.4 fusion.5
  131.5 0.5 fusion.4
  132.0 0.2 copy.58
  132.1 117.6 %all-gather.12.cloned.1.call-done = bf16[1024,4096]{1,0:T(8,128)(2,1)} async-done(((bf16[1024,512]{1,0:T(8,128)(2,1)}), bf16[1024,4096]{1,0:T(8,128)(2,1)}) %all-gather.12.cloned.1.call-update) | async-done | bytes 8388624 | tf_op jit(solution)/shard_map/all_gather | solution.py:110
  249.7 5.8 %convolution_convert_fusion = bf16[128,4096]{1,0:T(8,128)(2,1)} fusion(bf16[1024,4096]{1,0:T(8,128)(2,1)} %all-gather.12.cloned.1.call-done, bf16[16,8,8,128]{3,2,1,0:T(8,128)(2,1)S(1)} %bitcast.95), kind=kOutput, calls=%fused_computation.2 | convolution fusion | flops 1074266112 | bytes 9699328 | tf_op jit(solution)/shard_map/dot_general | solution.py:108
  255.5 6.7 %reduce-scatter.2.cloned.1.call-done = bf16[128,2048]{1,0:T(8,128)(2,1)} async-done(((bf16[128,4096]{1,0:T(8,128)(2,1)}), bf16[128,2048]{1,0:T(8,128)(2,1)}) %reduce-scatter.2.cloned.1.call-update) | async-done | bytes 524304 | tf_op jit(solution)/shard_map/reduce_scatter | solution.py:113
  262.2 2.0 add_convert_fusion
  (25 shorter events, 0.2 us)
Async XLA Ops:
  6.5 17.2 %copy-start = (bf16[1024,896]{1,0:T(8,128)(2,1)S(1)}, bf16[1024,896]{1,0:T(8,128)(2,1)}, u32[]{:S(2)}) copy-start(bf16[1024,896]{1,0:T(8,128)(2,1)} %param.12) | copy-start | bytes 5505028
  6.5 1.5 copy-start.4
  6.5 3.0 %copy-start.7 = (s32[2,2]{1,0:T(2,128)S(1)}, s32[2,2]{1,0:T(2,128)}, u32[]{:S(2)}) copy-start(s32[2,2]{1,0:T(2,128)} %param.13) | copy-start | bytes 52
  6.5 82.3 %all-gather.6.cloned.1.call-start = ((), (), s32[]{:S(2)}) async-start(), calls=%async_computation.3 | async-start | bytes 2408448 | tf_op jit(solution)/shard_map/all_gather | solution.py:81
  7.3 89.2 %all-gather.8.cloned.1.call-start = ((), (), s32[]{:S(2)}) async-start(), calls=%async_computation.4 | async-start | bytes 2408448 | tf_op jit(solution)/shard_map/all_gather | solution.py:82
  8.0 116.5 %all-gather.10.cloned.1.call-start = ((), (), s32[]{:S(2)}) async-start(), calls=%async_computation.5 | async-start | bytes 4128768 | tf_op jit(solution)/shard_map/all_gather | solution.py:93
  8.9 240.8 %all-gather.12.cloned.1.call-start = ((), (), s32[]{:S(2)}) async-start(), calls=%async_computation.6 | async-start | bytes 9437184 | tf_op jit(solution)/shard_map/all_gather | solution.py:110
  25.7 4.5 %copy-start.6 = (bf16[128,2,448]{0,2,1:T(8,128)(2,1)S(1)}, bf16[128,2,448]{0,2,1:T(8,128)(2,1)}, u32[]{:S(2)}) copy-start(bf16[128,2,448]{0,2,1:T(8,128)(2,1)} %param.11) | copy-start | bytes 688132
  25.7 60.7 %all-to-all-start.1 = ((bf16[8,1,128,896]{3,2,1,0:T(8,128)(2,1)}), bf16[8,1,128,896]{3,2,1,0:T(8,128)(2,1)}, u32[]{:S(2)}, u32[]{:S(2)}) async-start(bf16[8,1,128,896]{3,2,1,0:T(8,128)(2,1)} %bitcast.92), calls=%async_computation.1 | async-start | bytes 3670016 | tf_op jit(solution)/shard_map/all_to_all | solution.py:35
  30.2 232.1 %reduce-scatter.2.cloned.1.call-start = ((), (), s32[]{:S(2)}) async-start(), calls=%async_computation.7 | async-start | bytes 1572864 | tf_op jit(solution)/shard_map/reduce_scatter | solution.py:113
  32.4 3.2 %copy-start.5 = (bf16[128,1024]{1,0:T(8,128)(2,1)S(1)}, bf16[128,1024]{1,0:T(8,128)(2,1)}, u32[]{:S(2)}) copy-start(bf16[128,1024]{1,0:T(8,128)(2,1)} %param.10) | copy-start | bytes 786436
  93.7 2.0 copy-start.3
  129.5 1.0 copy-start.1
  249.7 12.5 %copy-start.2 = (bf16[128,2048]{1,0:T(8,128)(2,1)S(1)}, bf16[128,2048]{1,0:T(8,128)(2,1)}, u32[]{:S(2)}) copy-start(bf16[128,2048]{1,0:T(8,128)(2,1)} %param.9) | copy-start | bytes 1572868
Sparse Core Ops, SparseCore 0:
  8.9 12.5 all-gather.5
  23.0 11.0 all-gather.7
  36.1 88.3 all-gather.9
  126.4 123.2 all-gather.11
  255.6 6.5 reduce-scatter.1
where the time goes:
time: 271 us
  waiting for transfers between devices  199 us (73%)
  matrix products  18.5 us (7%)
  blocking collectives  18.2 us (7%)
  between operations  13.4 us (5%)
  local copies, waits for them, and re-layouts  13.1 us (5%)
  starting transfers between devices  4.61 us (2%)
  other arithmetic  3.53 us (1%)
    all_gather x1, waiting for transfers between devices, body(): lax.all_gather(out_weight, 'span', axis=1, tiled=True)  118 us
    all_to_all x1, waiting for transfers between devices, fetch_passages(): lax.all_to_all(picked, 'span', split_axis=0, concat_axis=0, tiled=True)  49.9 us
    all_gather x1, waiting for transfers between devices, body(): lax.all_gather(kv_weight, 'span', axis=2, tiled=True)  23.2 us
    all_to_all x1, blocking collectives, fetch_passages(): lax.all_to_all(wanted, 'span', split_axis=0, concat_axis=0, tiled=True)  13.6 us
    reduce_scatter x1, waiting for transfers between devices, body(): lax.psum_scatter(partial_value.astype(jnp.bfloat16), 'head', scatter_dime...  6.73 us
    dot_general x1, matrix products, body(): jnp.dot(attended, lax.all_gather(out_weight, 'span', axis=1, tiled=True),...  5.75 us
  transfers between devices with their start and end apart: 6, of which 4 were waited for; matrix products, arithmetic and copies ran while one was open for 10% of the time, Pallas kernels for 0%

commit v1 on v0

--- a/solution.py
+++ b/solution.py
@@ -12,6 +12,25 @@
 NB = 2
 PS_DEV = 8
 epsilon = 1e-06
+
+
+def in_order(blocks, dim):
+    blocks = jnp.moveaxis(blocks, 0, dim)
+    shape = blocks.shape
+    return blocks.reshape(*shape[:dim], shape[dim] * shape[dim + 1], *shape[dim + 2 :])
+
+
+def ring_apply(x, axis, dim, work, out_dim):
+    size, position, extent = (lax.axis_size(axis), lax.axis_index(axis), x.shape[dim])
+    right = [(i, (i + 1) % size) for i in range(size)]
+    blocks = []
+    held = x
+    for step in range(size):
+        coming = held if step == size - 1 else lax.ppermute(held, axis, right)
+        blocks.append(work(held, (position - step) % size * extent))
+        held = coming
+    blocks = jnp.stack(blocks)[(position - jnp.arange(size)) % size]
+    return in_order(blocks, out_dim)
 
 
 def rms_rows(values):
@@ -87,11 +106,14 @@
     encoded = rms_rows(own_rows + own_branch).astype(jnp.bfloat16)
     all_encoded = lax.all_gather(encoded[None], "head", axis=0, tiled=True)
     flat_encoded = all_encoded.reshape(-1, E)
-    dec_kv = jnp.einsum(
-        "re,esc->rsc",
-        flat_encoded,
-        lax.all_gather(kv_weight, "span", axis=2, tiled=True),
-        preferred_element_type=jnp.float32,
+    dec_kv = ring_apply(
+        kv_weight,
+        "span",
+        2,
+        lambda shard, at: jnp.einsum(
+            "re,esc->rsc", flat_encoded, shard, preferred_element_type=jnp.float32
+        ),
+        2,
     ).astype(jnp.bfloat16)
     head_count = span_queries.shape[1] // HD
     dec_kv = dec_kv.reshape(NB, span_count, PT, 2, head_count, HD)

time: 271 us -> 294 us (1.085)
  starting transfers between devices: 4.61 us -> 20.7 us
  matrix products: 18.5 us -> 27.5 us
  waiting for transfers between devices: 199 us -> 191 us
  local copies, waits for them, and re-layouts: 13.1 us -> 18.6 us
    ppermute x0 -> x7, waiting for transfers between devices: none -> 159 us  [ring_apply(): coming = held if step == size - 1 else lax.ppermute(held, axis, right)]
    all_gather x1, waiting for transfers between devices: 118 us -> 0.02 us  [body(): lax.all_gather(out_weight, 'span', axis=1, tiled=True)]
    all_to_all x1, waiting for transfers between devices: 49.9 us -> 0.01 us  [fetch_passages(): lax.all_to_all(picked, 'span', split_axis=0, concat_axis=0, tiled=True)]
    all_gather x1 -> x0, waiting for transfers between devices: 23.2 us -> none  [body(): lax.all_gather(kv_weight, 'span', axis=2, tiled=True)]
    reduce_scatter x1, waiting for transfers between devices: 6.73 us -> 29.5 us  [body(): lax.psum_scatter(partial_value.astype(jnp.bfloat16), 'head', scatter_dime...]
    ppermute x0 -> x7, starting transfers between devices: none -> 16.1 us  [ring_apply(): coming = held if step == size - 1 else lax.ppermute(held, axis, right)]
    dot_general x1 -> x8, matrix products: 4.37 us -> 13.4 us  [body(): jnp.einsum('re,esc->rsc', flat_encoded, shard, preferred_element_type=jnp...]
    gather x0 -> x1, local copies, waits for them, and re-layouts: none -> 3.72 us  [ring_apply(): blocks = jnp.stack(blocks)[(position - jnp.arange(size)) % size]]
  transfers between devices with their start and end apart: 6 -> 12, of which waited for: 4 -> 7; matrix products, arithmetic and copies ran while one was open for 10% -> 13% of each run, Pallas kernels for 0% -> 0%
where the time goes in v1:
time: 294 us; the launch traced here: 293 us
  waiting for transfers between devices  191 us (65%)
  matrix products  27.5 us (9%)
  starting transfers between devices  20.7 us (7%)
  local copies, waits for them, and re-layouts  18.6 us (6%)
  blocking collectives  18.5 us (6%)
  between operations  13.4 us (5%)
  other arithmetic  3.54 us (1%)
    ppermute x7, waiting for transfers between devices, ring_apply(): coming = held if step == size - 1 else lax.ppermute(held, axis, right)  159 us
    reduce_scatter x1, waiting for transfers between devices, body(): lax.psum_scatter(partial_value.astype(jnp.bfloat16), 'head', scatter_dime...  29.5 us
    ppermute x7, starting transfers between devices, ring_apply(): coming = held if step == size - 1 else lax.ppermute(held, axis, right)  16.1 us
    all_to_all x1, blocking collectives, fetch_passages(): lax.all_to_all(wanted, 'span', split_axis=0, concat_axis=0, tiled=True)  13.6 us
    dot_general x8, matrix products, body(): jnp.einsum('re,esc->rsc', flat_encoded, shard, preferred_element_type=jnp...  13.4 us
  transfers between devices with their start and end apart: 12, of which 7 were waited for; matrix products, arithmetic and copies ran while one was open for 13% of the time, Pallas kernels for 0%

profile of v1, /device:TPU:0, one launch (start us, length us, event | category | flops | bytes accessed | tf_op | source)
XLA Modules:
  0.0 293.3 jit_solution(2058535495606247030)
XLA Ops:
  6.5 0.7 all-gather.5.cloned.1.call-update
  7.3 0.7 all-gather.7.cloned.1.call-update
  8.1 0.7 all-gather.9.cloned.1.call-update
  9.1 13.6 %all_to_all.14 = s32[8,1,1]{2,1,0:T(1,128)S(1)} all-to-all(s32[8,1,1]{2,1,0:T(1,128)S(1)} %copy.52), channel_id=1, replica_groups=mesh['groups'=2,'span'=8,'head'=2] {'span'}, dimensions={0} | all-to-all | bytes 64 | tf_op jit(solution)/shard_map/all_to_all | solution.py:53
  22.7 0.2 fusion.35
  23.0 2.0 gather_fusion
  25.0 4.5 %all-to-all-start.1 = ((bf16[8,1,128,896]{3,2,1,0:T(8,128)(2,1)}), bf16[8,1,128,896]{3,2,1,0:T(8,128)(2,1)}, u32[]{:S(2)}, u32[]{:S(2)}) async-start(bf16[8,1,128,896]{3,2,1,0:T(8,128)(2,1)} %bitcast.143), calls=%async_computation.1 | async-start | bytes 3670016 | tf_op jit(solution)/shard_map/all_to_all | solution.py:54
  29.6 1.9 collective-permute-start
  31.5 64.0 %collective-permute-done = bf16[896,2,128]{2,0,1:T(8,128)(2,1)S(1)} collective-permute-done((bf16[896,2,128]{2,0,1:T(8,128)(2,1)S(1)}, bf16[896,2,128]{2,0,1:T(8,128)(2,1)S(1)}, u32[]{:S(2)}, u32[]{:S(2)}) %collective-permute-start) | collective-permute-done | bytes 458784 | tf_op jit(solution)/shard_map/ppermute | solution.py:29
  95.5 0.8 copy-done.6
  96.3 22.4 %collective-permute-done.1 = bf16[896,2,128]{2,0,1:T(8,128)(2,1)S(1)} collective-permute-done((bf16[896,2,128]{2,0,1:T(8,128)(2,1)S(1)}, bf16[896,2,128]{2,0,1:T(8,128)(2,1)S(1)}, u32[]{:S(2)}, u32[]{:S(2)}) %collective-permute-start.1) | collective-permute-done | bytes 458784 | tf_op jit(solution)/shard_map/ppermute | solution.py:29
  118.7 0.8 copy-done.8
  119.5 15.0 %collective-permute-done.2 = bf16[896,2,128]{2,0,1:T(8,128)(2,1)S(1)} collective-permute-done((bf16[896,2,128]{2,0,1:T(8,128)(2,1)S(1)}, bf16[896,2,128]{2,0,1:T(8,128)(2,1)S(1)}, u32[]{:S(2)}, u32[]{:S(2)}) %collective-permute-start.2) | collective-permute-done | bytes 458784 | tf_op jit(solution)/shard_map/ppermute | solution.py:29
  134.5 0.8 copy-done.10
  135.2 19.8 %collective-permute-done.3 = bf16[896,2,128]{2,0,1:T(8,128)(2,1)} collective-permute-done((bf16[896,2,128]{2,0,1:T(8,128)(2,1)S(1)}, bf16[896,2,128]{2,0,1:T(8,128)(2,1)}, u32[]{:S(2)}, u32[]{:S(2)}) %collective-permute-start.3) | collective-permute-done | bytes 458784 | tf_op jit(solution)/shard_map/ppermute | solution.py:29
  155.1 2.1 all_gather.16
  157.2 0.4 reshape.141
  157.6 1.7 fusion.43
  159.3 1.1 copy.71
  160.6 16.0 %collective-permute-done.4 = bf16[896,2,128]{2,0,1:T(8,128)(2,1)} collective-permute-done((bf16[896,2,128]{2,0,1:T(8,128)(2,1)}, bf16[896,2,128]{2,0,1:T(8,128)(2,1)}, u32[]{:S(2)}, u32[]{:S(2)}) %collective-permute-start.4) | collective-permute-done | bytes 458784 | tf_op jit(solution)/shard_map/ppermute | solution.py:29
  176.6 0.4 collective-permute-start.5
  177.0 0.7 bitcast_bitcast_fusion
  177.7 22.1 %collective-permute-done.5 = bf16[896,2,128]{2,0,1:T(8,128)(2,1)} collective-permute-done((bf16[896,2,128]{2,0,1:T(8,128)(2,1)}, bf16[896,2,128]{2,0,1:T(8,128)(2,1)}, u32[]{:S(2)}, u32[]{:S(2)}) %collective-permute-start.5) | collective-permute-done | bytes 458784 | tf_op jit(solution)/shard_map/ppermute | solution.py:29
  199.8 13.8 %collective-permute-start.6 = (bf16[896,2,128]{2,0,1:T(8,128)(2,1)}, bf16[896,2,128]{2,0,1:T(8,128)(2,1)}, u32[]{:S(2)}, u32[]{:S(2)}) collective-permute-start(bf16[896,2,128]{2,0,1:T(8,128)(2,1)} %collective-permute-done.5), channel_id=1, source_target_pairs={{0,2},{2,4},{4,6},{6,8},{8,10},{10,12},{12,14},{14,0},{1,3},{3,5},... | collective-permute-start | bytes 1376264 | tf_op jit(solution)/shard_map/ppermute | solution.py:29
  213.6 2.2 gather_fusion.1
  216.1 3.0 %convolution_convert_fusion.2 = bf16[256,896]{1,0:T(8,128)(2,1)} fusion(bf16[256,896]{1,0:T(8,128)(2,1)S(1)} %fusion.23, bf16[896,896]{0,1:T(8,128)(2,1)} %all-gather.5.cloned.1.call-done), kind=kOutput, calls=%fused_computation.10 | convolution fusion | flops 411271168 | bytes 2523136 | tf_op jit(solution)/shard_map/dot_general | solution.py:63
  219.1 1.8 reshape.175
  220.9 1.8 fusion.44
  222.9 0.3 fusion.10
  223.2 0.5 copy.57
  223.7 2.2 multiply_reduce_fusion
  226.1 2.8 all-gather
  228.9 1.2 fusion.9
  230.1 1.2 fusion.8
  231.3 1.1 fusion.7
  232.5 1.2 fusion.6
  233.6 2.2 fusion.5
  235.8 2.2 fusion.4
  238.0 2.2 fusion.3
  240.1 2.2 fusion.2
  242.3 3.7 %gather_fusion.2 = bf16[8,512,2,128]{3,1,2,0:T(8,128)(2,1)} fusion(bf16[8,512,2,128]{3,1,2,0:T(8,128)(2,1)} %fusion.2, s32[1024]{0:T(1024)S(1)} %pad_clamp_fusion), kind=kCustom, calls=%fused_computation.2 | custom fusion | bytes 4194336 | tf_op jit(solution)/shard_map/gather | solution.py:32
  246.0 1.7 fusion.42
  247.8 0.6 fusion.45
  248.3 0.4 fusion.13
  248.7 0.5 fusion.12
  249.5 5.8 %convolution_convert_fusion = bf16[128,4096]{1,0:T(8,128)(2,1)} fusion(bf16[1024,4096]{1,0:T(8,128)(2,1)} %all-gather.9.cloned.1.call-done, bf16[16,8,8,128]{3,2,1,0:T(8,128)(2,1)S(1)} %bitcast.145), kind=kOutput, calls=%fused_computation.3 | convolution fusion | flops 1074266112 | bytes 9699328 | tf_op jit(solution)/shard_map/dot_general | solution.py:130
  255.2 29.5 %reduce-scatter.2.cloned.1.call-done = bf16[128,2048]{1,0:T(8,128)(2,1)} async-done(((bf16[128,4096]{1,0:T(8,128)(2,1)}), bf16[128,2048]{1,0:T(8,128)(2,1)}) %reduce-scatter.2.cloned.1.call-update) | async-done | bytes 524304 | tf_op jit(solution)/shard_map/reduce_scatter | solution.py:135
  284.8 2.0 add_convert_fusion
  (59 shorter events, 1.7 us)
Async XLA Ops:
  6.5 16.4 %copy-start = (bf16[1024,896]{1,0:T(8,128)(2,1)S(1)}, bf16[1024,896]{1,0:T(8,128)(2,1)}, u32[]{:S(2)}) copy-start(bf16[1024,896]{1,0:T(8,128)(2,1)} %param.12) | copy-start | bytes 5505028
  6.5 2.2 copy-start.14
  6.5 209.6 %all-gather.5.cloned.1.call-start = ((), (), s32[]{:S(2)}) async-start(), calls=%async_computation.3 | async-start | bytes 2408448 | tf_op jit(solution)/shard_map/all_gather | solution.py:100
  7.3 216.5 %all-gather.7.cloned.1.call-start = ((), (), s32[]{:S(2)}) async-start(), calls=%async_computation.4 | async-start | bytes 2408448 | tf_op jit(solution)/shard_map/all_gather | solution.py:101
  8.0 241.4 %all-gather.9.cloned.1.call-start = ((), (), s32[]{:S(2)}) async-start(), calls=%async_computation.5 | async-start | bytes 9437184 | tf_op jit(solution)/shard_map/all_gather | solution.py:132
  25.0 4.5 %copy-start.4 = (bf16[896,2,128]{2,1,0:T(2,128)(2,1)S(1)}, bf16[896,2,128]{2,1,0:T(2,128)(2,1)}, u32[]{:S(2)}) copy-start(bf16[896,2,128]{2,1,0:T(2,128)(2,1)} %param.16) | copy-start | bytes 1376260
  25.0 130.1 %copy-start.13 = (bf16[128,2,448]{0,2,1:T(8,128)(2,1)S(1)}, bf16[128,2,448]{0,2,1:T(8,128)(2,1)}, u32[]{:S(2)}) copy-start(bf16[128,2,448]{0,2,1:T(8,128)(2,1)} %param.11) | copy-start | bytes 688132
  25.0 188.7 %all-to-all-start.1 = ((bf16[8,1,128,896]{3,2,1,0:T(8,128)(2,1)}), bf16[8,1,128,896]{3,2,1,0:T(8,128)(2,1)}, u32[]{:S(2)}, u32[]{:S(2)}) async-start(bf16[8,1,128,896]{3,2,1,0:T(8,128)(2,1)} %bitcast.143), calls=%async_computation.1 | async-start | bytes 3670016 | tf_op jit(solution)/shard_map/all_to_all | solution.py:54
  29.4 255.3 %reduce-scatter.2.cloned.1.call-start = ((), (), s32[]{:S(2)}) async-start(), calls=%async_computation.6 | async-start | bytes 1572864 | tf_op jit(solution)/shard_map/reduce_scatter | solution.py:135
  29.6 65.9 %collective-permute-start = (bf16[896,2,128]{2,0,1:T(8,128)(2,1)S(1)}, bf16[896,2,128]{2,0,1:T(8,128)(2,1)S(1)}, u32[]{:S(2)}, u32[]{:S(2)}) collective-permute-start(bf16[896,2,128]{2,0,1:T(8,128)(2,1)S(1)} %copy.58), channel_id=1, source_target_pairs={{0,2},{2,4},{4,6},{6,8},{8,10},{10,12},{12,14},{14,0},{1,3},{3,5},... | collective-permute-start | bytes 1376264 | tf_op jit(solution)/shard_map/ppermute | solution.py:29
  95.5 0.8 copy-start.6
  96.3 22.4 %collective-permute-start.1 = (bf16[896,2,128]{2,0,1:T(8,128)(2,1)S(1)}, bf16[896,2,128]{2,0,1:T(8,128)(2,1)S(1)}, u32[]{:S(2)}, u32[]{:S(2)}) collective-permute-start(bf16[896,2,128]{2,0,1:T(8,128)(2,1)S(1)} %collective-permute-done), channel_id=1, source_target_pairs={{0,2},{2,4},{4,6},{6,8},{8,10},{10,12},{12,14},{14,0},{1,3},{3,5},... | collective-permute-start | bytes 1376264 | tf_op jit(solution)/shard_map/ppermute | solution.py:29
  118.7 0.8 copy-start.8
  119.5 15.0 %collective-permute-start.2 = (bf16[896,2,128]{2,0,1:T(8,128)(2,1)S(1)}, bf16[896,2,128]{2,0,1:T(8,128)(2,1)S(1)}, u32[]{:S(2)}, u32[]{:S(2)}) collective-permute-start(bf16[896,2,128]{2,0,1:T(8,128)(2,1)S(1)} %collective-permute-done.1), channel_id=1, source_target_pairs={{0,2},{2,4},{4,6},{6,8},{8,10},{10,12},{12,14},{14,0},{1,3},{3,5},... | collective-permute-start | bytes 1376264 | tf_op jit(solution)/shard_map/ppermute | solution.py:29
  134.5 0.8 copy-start.10
  135.2 19.8 %collective-permute-start.3 = (bf16[896,2,128]{2,0,1:T(8,128)(2,1)S(1)}, bf16[896,2,128]{2,0,1:T(8,128)(2,1)}, u32[]{:S(2)}, u32[]{:S(2)}) collective-permute-start(bf16[896,2,128]{2,0,1:T(8,128)(2,1)S(1)} %collective-permute-done.2), channel_id=1, source_target_pairs={{0,2},{2,4},{4,6},{6,8},{8,10},{10,12},{12,14},{14,0},{1,3},{3,5},... | collective-permute-start | bytes 1376264 | tf_op jit(solution)/shard_map/ppermute | solution.py:29
  155.0 21.5 %collective-permute-start.4 = (bf16[896,2,128]{2,0,1:T(8,128)(2,1)}, bf16[896,2,128]{2,0,1:T(8,128)(2,1)}, u32[]{:S(2)}, u32[]{:S(2)}) collective-permute-start(bf16[896,2,128]{2,0,1:T(8,128)(2,1)} %collective-permute-done.3), channel_id=1, source_target_pairs={{0,2},{2,4},{4,6},{6,8},{8,10},{10,12},{12,14},{14,0},{1,3},{3,5},... | collective-permute-start | bytes 1376264 | tf_op jit(solution)/shard_map/ppermute | solution.py:29
  157.2 3.1 %copy-start.12 = (bf16[128,1024]{1,0:T(8,128)(2,1)S(1)}, bf16[128,1024]{1,0:T(8,128)(2,1)}, u32[]{:S(2)}) copy-start(bf16[128,1024]{1,0:T(8,128)(2,1)} %param.10) | copy-start | bytes 786436
  176.6 23.2 %collective-permute-start.5 = (bf16[896,2,128]{2,0,1:T(8,128)(2,1)}, bf16[896,2,128]{2,0,1:T(8,128)(2,1)}, u32[]{:S(2)}, u32[]{:S(2)}) collective-permute-start(bf16[896,2,128]{2,0,1:T(8,128)(2,1)} %collective-permute-done.4), channel_id=1, source_target_pairs={{0,2},{2,4},{4,6},{6,8},{8,10},{10,12},{12,14},{14,0},{1,3},{3,5},... | collective-permute-start | bytes 1376264 | tf_op jit(solution)/shard_map/ppermute | solution.py:29
  199.8 40.3 %collective-permute-start.6 = (bf16[896,2,128]{2,0,1:T(8,128)(2,1)}, bf16[896,2,128]{2,0,1:T(8,128)(2,1)}, u32[]{:S(2)}, u32[]{:S(2)}) collective-permute-start(bf16[896,2,128]{2,0,1:T(8,128)(2,1)} %collective-permute-done.5), channel_id=1, source_target_pairs={{0,2},{2,4},{4,6},{6,8},{8,10},{10,12},{12,14},{14,0},{1,3},{3,5},... | collective-permute-start | bytes 1376264 | tf_op jit(solution)/shard_map/ppermute | solution.py:29
  220.9 2.0 copy-start.3
  226.0 2.9 %copy-start.5 = (bf16[896,2,128]{2,1,0:T(2,128)(2,1)S(1)}, bf16[896,2,128]{2,1,0:T(2,128)(2,1)}, u32[]{:S(2)}) copy-start(bf16[896,2,128]{2,1,0:T(2,128)(2,1)} %param.16) | copy-start | bytes 1376260
  226.0 4.1 %copy-start.7 = (bf16[896,2,128]{2,0,1:T(8,128)(2,1)S(1)}, bf16[896,2,128]{2,0,1:T(8,128)(2,1)}, u32[]{:S(2)}) copy-start(bf16[896,2,128]{2,0,1:T(8,128)(2,1)} %copy-done.6) | copy-start | bytes 1376260
  228.9 2.4 copy-start.9
  230.1 2.3 copy-start.11
  246.0 1.7 copy-start.1
  249.4 35.3 %copy-start.2 = (bf16[128,2048]{1,0:T(8,128)(2,1)S(1)}, bf16[128,2048]{1,0:T(8,128)(2,1)}, u32[]{:S(2)}) copy-start(bf16[128,2048]{1,0:T(8,128)(2,1)} %param.9) | copy-start | bytes 1572868
Sparse Core Ops, SparseCore 0:
  8.9 12.5 all-gather.4
  23.0 11.0 all-gather.6
  36.1 201.6 all-gather.8
  255.4 29.3 reduce-scatter.1
